TPU v7x, 128 devices: a whole 4x4x4 slice. The times are simulated.
128 devices in a mesh: space: 16 (over y_hi, x, core), code: 4 (over z), clip: 2 (over y_lo).
Axes of the slice: x: 4, y: 4 (y_hi: 2, y_lo: 2; y = y_hi * 2 + y_lo), z: 4, core: 2. Of those that a mesh axis runs over, the one named last changes fastest.
Arguments:
- soft_weights: bfloat16 [2, 1024, 32, 8192], P('clip', 'space', None, 'code'), may hold values from 0.00029945374 to 0.029907227
- codebook: bfloat16 [8192, 256], P('code'), may hold values from -6 to 6
- kernel_one: bfloat16 [3, 3, 256, 512], replicated, may hold values from -0.125 to 0.125
- kernel_two: bfloat16 [3, 3, 512, 512], replicated, may hold values from -0.09375 to 0.09375
- cotangent: bfloat16 [2, 1024, 32, 512], P('clip', ('space', 'code')), may hold values from -16 to 16
Outputs:
- decoded: bfloat16 [2, 1024, 32, 512], P('clip', ('space', 'code'))
- grad_one: float32 [3, 3, 256, 512], P(None, None, None, ('space', 'code', 'clip'))
- grad_two: float32 [3, 3, 512, 512], P(None, None, None, ('space', 'code', 'clip'))
- grad_codebook: float32 [8192, 256], P('code')
All inputs are finite; a program needn't handle non-finite values.
Results may differ from a plain program's by a relative error of at most 0.02.
Values may be sent and summed in bfloat16 or wider, within the bound.
A program may use at most 192 MiB of HBM per device.

v0:
```python
import jax
import jax.numpy as jnp
from jax import lax
from jax.sharding import PartitionSpec as P


def with_halo(block, sides, width):
    for axis, dim in sides:
        count = lax.axis_size(axis)
        forward = [(i, i + 1) for i in range(count - 1)]
        backward = [(target, source) for source, target in forward]
        low = lax.ppermute(
            lax.slice_in_dim(block, block.shape[dim] - width, None, axis=dim), axis, forward
        )
        high = lax.ppermute(lax.slice_in_dim(block, 0, width, axis=dim), axis, backward)
        block = jnp.concatenate([low, block, high], axis=dim)
    return block


def extend(field):
    grown = with_halo(field, ((("space", "code"), 0),), 1)
    return jnp.pad(grown, ((0, 0), (1, 1), (0, 0)))


def taps_forward(padded, kernel):
    height = padded.shape[0] - 2
    breadth = padded.shape[1] - 2
    accum = jnp.zeros((height * breadth, kernel.shape[3]), jnp.float32)
    for first in range(3):
        for second in range(3):
            window = padded[first : first + height, second : second + breadth].reshape(
                height * breadth, -1
            )
            accum = accum + jnp.dot(
                window, kernel[first, second], preferred_element_type=jnp.float32
            )
    return accum.reshape(height, breadth, -1)


def taps_back(padded, kernel):
    height = padded.shape[0] - 2
    breadth = padded.shape[1] - 2
    accum = jnp.zeros((height * breadth, kernel.shape[2]), jnp.float32)
    for first in range(3):
        for second in range(3):
            window = padded[
                2 - first : 2 - first + height, 2 - second : 2 - second + breadth
            ].reshape(height * breadth, -1)
            accum = accum + jnp.dot(
                window, kernel[first, second].T, preferred_element_type=jnp.float32
            )
    return accum.reshape(height, breadth, -1)


def kernel_grad(padded, upstream):
    height = upstream.shape[0]
    breadth = upstream.shape[1]
    flat_up = upstream.reshape(height * breadth, -1)
    result = []
    for first in range(3):
        line = []
        for second in range(3):
            window = padded[first : first + height, second : second + breadth].reshape(
                height * breadth, -1
            )
            line.append(
                lax.dot_general(
                    window, flat_up, (((0,), (0,)), ((), ())), preferred_element_type=jnp.float32
                )
            )
        result.append(jnp.stack(line))
    return jnp.stack(result)


def on_device(soft_weights, codebook, kernel_one, kernel_two, cotangent):
    weights = soft_weights[0]
    upstream = cotangent[0]
    own_rows = upstream.shape[0]
    breadth = weights.shape[1]
    code_slice = weights.shape[2]
    partial_value = jnp.dot(
        weights.reshape(-1, code_slice), codebook, preferred_element_type=jnp.float32
    )
    partial_value = partial_value.reshape(weights.shape[0], breadth, -1)
    summed = lax.psum(partial_value, "code")
    owned = lax.dynamic_slice_in_dim(summed, lax.axis_index("code") * own_rows, own_rows, 0)
    embedded = owned.astype(jnp.bfloat16)
    embed_pad = extend(embedded)
    pre_one = taps_forward(embed_pad, kernel_one)
    hidden = jax.nn.silu(pre_one).astype(jnp.bfloat16)
    hidden_pad = extend(hidden)
    decoded = taps_forward(hidden_pad, kernel_two).astype(jnp.bfloat16)
    grad_hidden = taps_back(extend(upstream), kernel_two)
    sigma = jax.nn.sigmoid(pre_one)
    grad_pre = (grad_hidden * sigma * (1.0 + pre_one * (1.0 - sigma))).astype(jnp.bfloat16)
    grad_embedded = taps_back(extend(grad_pre), kernel_one).astype(jnp.bfloat16)
    piece = lax.all_gather(grad_embedded, "code", axis=0, tiled=True)
    code_terms = lax.dot_general(
        weights.reshape(-1, code_slice),
        piece.reshape(-1, piece.shape[2]),
        (((0,), (0,)), ((), ())),
        preferred_element_type=jnp.float32,
    )
    grad_codebook = lax.psum(code_terms.astype(jnp.bfloat16), ("space", "clip")).astype(jnp.float32)
    term_two = kernel_grad(hidden_pad, upstream)
    term_one = kernel_grad(embed_pad, grad_pre)
    grad_one, grad_two = (
        lax.psum_scatter(term_one, ("space", "code", "clip"), scatter_dimension=3, tiled=True),
        lax.psum_scatter(term_two, ("space", "code", "clip"), scatter_dimension=3, tiled=True),
    )
    return (decoded[None], grad_one, grad_two, grad_codebook)


def solution(mesh):
    in_specs = (
        P("clip", "space", None, "code"),
        P("code", None),
        P(),
        P(),
        P("clip", ("space", "code"), None, None),
    )
    out_specs = (
        P("clip", ("space", "code"), None, None),
        P(None, None, None, ("space", "code", "clip")),
        P(None, None, None, ("space", "code", "clip")),
        P("code", None),
    )
    return jax.shard_map(
        on_device, mesh=mesh, in_specs=in_specs, out_specs=out_specs, check_vma=False
    )
```

profile of v0, /device:TPU:1, one launch (start us, length us, event | category | flops | bytes accessed | tf_op | source)
XLA Modules:
  0.0 509.3 jit_solution(13997313864569233537)
XLA Ops:
  8.4 5.7 %fusion = f32[64,32,256]{2,1,0:T(8,128)S(1)} fusion(bf16[1,64,32,2048]{3,2,1,0:T(8,128)(2,1)} %param.5, bf16[2048,256]{1,0:T(8,128)(2,1)S(1)} %copy-done), kind=kOutput, calls=%fused_computation.1 | convolution fusion | flops 2147483648 | bytes 11534336 | tf_op jit(solution)/shard_map/dot_general | solution.py:81
  14.1 44.1 %all-reduce.14 = bf16[64,32,256]{2,1,0:T(8,128)(2,1)} all-reduce(f32[64,32,256]{2,1,0:T(8,128)S(1)} %fusion), channel_id=1, replica_groups=mesh['space'=16,'code'=4,'clip'=2] {'code'}, use_global_device_ids=true, to_apply=%region_0.0 | all-reduce | flops 524288 | bytes 3145728 | tf_op jit(solution)/shard_map/psum | solution.py:85
  59.4 1.9 collective-permute-start
  61.3 5.2 %collective-permute-start.1 = (bf16[1,32,256]{2,1,0:T(8,128)(2,1)S(1)}, bf16[1,32,256]{2,1,0:T(8,128)(2,1)S(1)}, u32[]{:S(2)}, u32[]{:S(2)}) collective-permute-start(bf16[1,32,256]{2,1,0:T(8,128)(2,1)S(1)} %get-tuple-element.55), channel_id=1, source_target_pairs={{2,0},{4,2},{6,4},{8,6},{10,8},{12,10},{14,12},{16,14},{18,16},{20... | collective-permute-start | bytes 49160 | tf_op jit(solution)/shard_map/ppermute | solution.py:15
  66.5 1.9 collective-permute-start.4
  68.5 4.9 collective-permute-start.5
  76.5 1.5 convolution_bitcast_fusion.4
  88.3 1.9 collective-permute-start.2
  90.2 4.9 collective-permute-start.3
  95.0 1.9 collective-permute-start.6
  97.0 5.0 collective-permute-start.7
  103.2 2.7 pad_maximum_fusion.1
  105.8 7.3 %copy.12 = f32[3,3,256,512]{2,1,0,3:T(4,128)} copy(f32[3,3,256,512]{3,2,1,0:T(8,128)} %pad_maximum_fusion.1) | data formatting | bytes 9437184 | tf_op jit(solution)/shard_map/stack | solution.py:72
  113.4 2.0 fusion.114
  127.8 3.4 maximum_bitcast_fusion
  131.2 27.6 %all-gather.2.cloned.1.call-done = bf16[64,32,256]{2,1,0:T(8,128)(2,1)} async-done(((bf16[16,32,256]{2,1,0:T(8,128)(2,1)}), bf16[64,32,256]{2,1,0:T(8,128)(2,1)}) %all-gather.2.cloned.1.call-update) | async-done | bytes 1048592 | tf_op jit(solution)/shard_map/all_gather | solution.py:97
  158.8 7.0 %fusion.2 = bf16[2048,256]{0,1:T(8,128)(2,1)} fusion(bf16[2048,256]{1,0:T(8,128)(2,1)} %bitcast.297, bf16[2048,2048]{1,0:T(8,128)(2,1)} %bitcast.275), kind=kOutput, calls=%fused_computation.8 | convolution fusion | flops 2148007936 | bytes 10485760 | tf_op jit(solution)/shard_map/dot_general | solution.py:98
  166.1 2.3 maximum_bitcast_fusion.2
  169.9 4.7 pad_maximum_fusion
  174.6 13.8 %copy.13 = f32[3,3,512,512]{2,1,0,3:T(4,128)} copy(f32[3,3,512,512]{3,2,1,0:T(8,128)} %pad_maximum_fusion) | data formatting | bytes 18874368 | tf_op jit(solution)/shard_map/stack | solution.py:72
  188.5 1.7 fusion.32
  190.2 1.5 fusion.14
  191.7 1.5 convolution_add_fusion.13
  193.2 1.5 convolution_add_fusion.12
  194.7 1.6 convolution_add_fusion.11
  196.3 1.5 convolution_add_fusion.10
  197.8 1.5 convolution_add_fusion.9
  199.3 1.5 convolution_add_fusion.8
  200.8 2.4 fusion.7
  203.2 70.1 %all-reduce.11.cloned.1.call-done = bf16[2048,256]{0,1:T(8,128)(2,1)} async-done(((bf16[2048,256]{0,1:T(8,128)(2,1)}), bf16[2048,256]{0,1:T(8,128)(2,1)}) %all-reduce.11.cloned.1.call-update) | async-done | bytes 1048592 | tf_op jit(solution)/shard_map/psum | solution.py:104
  273.2 2.6 copy.16
  275.8 223.9 %all-reduce.13.cloned.1.call-done = (f32[3,3,256,512]{2,1,0,3:T(4,128)}, f32[3,3,512,512]{2,1,0,3:T(4,128)}) async-done(((f32[3,3,256,512]{2,1,0,3:T(4,128)}, f32[3,3,512,512]{2,1,0,3:T(4,128)}), (f32[3,3,256,512]{2,1,0,3:T(4,128)}, f32[3,3,512,512]{2,1,0,3:T(4,128)})) %all-reduce.13.cloned.1.call-update) | async-done | bytes 14155792
  (136 shorter events, 33.8 us)
Async XLA Ops:
  7.2 151.6 %all-gather.2.cloned.1.call-start = ((), (), s32[]{:S(2)}) async-start(), calls=%async_computation | async-start | bytes 1310720 | tf_op jit(solution)/shard_map/all_gather | solution.py:97
  14.1 52.4 %copy-start.2 = (bf16[1,16,32,512]{3,2,1,0:T(8,128)(2,1)S(1)}, bf16[1,16,32,512]{3,2,1,0:T(8,128)(2,1)}, u32[]{:S(2)}) copy-start(bf16[1,16,32,512]{3,2,1,0:T(8,128)(2,1)} %param.9) | copy-start | bytes 1572868
  58.3 15.5 %copy-start.5 = (bf16[3,3,256,512]{3,2,1,0:T(8,128)(2,1)S(1)}, bf16[3,3,256,512]{3,2,1,0:T(8,128)(2,1)}, u32[]{:S(2)}) copy-start(bf16[3,3,256,512]{3,2,1,0:T(8,128)(2,1)} %param.7) | copy-start | bytes 7077892
  59.4 13.9 %collective-permute-start = (bf16[1,32,256]{2,1,0:T(8,128)(2,1)S(1)}, bf16[1,32,256]{2,1,0:T(8,128)(2,1)S(1)}, u32[]{:S(2)}, u32[]{:S(2)}) collective-permute-start(bf16[1,32,256]{2,1,0:T(8,128)(2,1)S(1)} %get-tuple-element.54), channel_id=1, source_target_pairs={{0,2},{2,4},{4,6},{6,8},{8,10},{10,12},{12,14},{14,16},{16,18},{18... | collective-permute-start | bytes 49160 | tf_op jit(solution)/shard_map/ppermute | solution.py:12
  61.3 12.0 %collective-permute-start.1 = (bf16[1,32,256]{2,1,0:T(8,128)(2,1)S(1)}, bf16[1,32,256]{2,1,0:T(8,128)(2,1)S(1)}, u32[]{:S(2)}, u32[]{:S(2)}) collective-permute-start(bf16[1,32,256]{2,1,0:T(8,128)(2,1)S(1)} %get-tuple-element.55), channel_id=1, source_target_pairs={{2,0},{4,2},{6,4},{8,6},{10,8},{12,10},{14,12},{16,14},{18,16},{20... | collective-permute-start | bytes 49160 | tf_op jit(solution)/shard_map/ppermute | solution.py:15
  66.5 11.5 %collective-permute-start.4 = (bf16[1,32,512]{2,1,0:T(8,128)(2,1)S(1)}, bf16[1,32,512]{2,1,0:T(8,128)(2,1)S(1)}, u32[]{:S(2)}, u32[]{:S(2)}) collective-permute-start(bf16[1,32,512]{2,1,0:T(8,128)(2,1)S(1)} %get-tuple-element.40), channel_id=1, source_target_pairs={{0,2},{2,4},{4,6},{6,8},{8,10},{10,12},{12,14},{14,16},{16,18},{18... | collective-permute-start | bytes 98312 | tf_op jit(solution)/shard_map/ppermute | solution.py:12
  68.5 9.6 %collective-permute-start.5 = (bf16[1,32,512]{2,1,0:T(8,128)(2,1)S(1)}, bf16[1,32,512]{2,1,0:T(8,128)(2,1)S(1)}, u32[]{:S(2)}, u32[]{:S(2)}) collective-permute-start(bf16[1,32,512]{2,1,0:T(8,128)(2,1)S(1)} %get-tuple-element.41), channel_id=1, source_target_pairs={{2,0},{4,2},{6,4},{8,6},{10,8},{12,10},{14,12},{16,14},{18,16},{20... | collective-permute-start | bytes 98312 | tf_op jit(solution)/shard_map/ppermute | solution.py:15
  76.5 7.6 %copy-start.19 = (f32[512,512]{1,0:T(8,128)}, f32[512,512]{1,0:T(8,128)S(1)}, u32[]{:S(2)}) copy-start(f32[512,512]{1,0:T(8,128)S(1)} %fusion.6) | copy-start | bytes 3145732
  76.5 2.9 slice-start
  78.0 1.7 slice-start.1
  84.6 3.0 copy-start.6
  84.6 17.8 %copy-start.8 = (bf16[16,32,512]{2,1,0:T(8,128)(2,1)}, bf16[16,32,512]{2,1,0:T(8,128)(2,1)S(1)}, u32[]{:S(2)}) copy-start(bf16[16,32,512]{2,1,0:T(8,128)(2,1)S(1)} %get-tuple-element.14) | copy-start | bytes 1572868
  88.3 24.8 %collective-permute-start.2 = (bf16[1,32,512]{2,1,0:T(8,128)(2,1)}, bf16[1,32,512]{2,1,0:T(8,128)(2,1)S(1)}, u32[]{:S(2)}, u32[]{:S(2)}) collective-permute-start(bf16[1,32,512]{2,1,0:T(8,128)(2,1)} %get-tuple-element.44), channel_id=1, source_target_pairs={{0,2},{2,4},{4,6},{6,8},{8,10},{10,12},{12,14},{14,16},{16,18},{18... | collective-permute-start | bytes 98312 | tf_op jit(solution)/shard_map/ppermute | solution.py:12
  90.2 22.9 %collective-permute-start.3 = (bf16[1,32,512]{2,1,0:T(8,128)(2,1)}, bf16[1,32,512]{2,1,0:T(8,128)(2,1)S(1)}, u32[]{:S(2)}, u32[]{:S(2)}) collective-permute-start(bf16[1,32,512]{2,1,0:T(8,128)(2,1)} %get-tuple-element.45), channel_id=1, source_target_pairs={{2,0},{4,2},{6,4},{8,6},{10,8},{12,10},{14,12},{16,14},{18,16},{20... | collective-permute-start | bytes 98312 | tf_op jit(solution)/shard_map/ppermute | solution.py:15
  95.0 20.3 %collective-permute-start.6 = (bf16[1,32,512]{2,1,0:T(8,128)(2,1)}, bf16[1,32,512]{2,1,0:T(8,128)(2,1)S(1)}, u32[]{:S(2)}, u32[]{:S(2)}) collective-permute-start(bf16[1,32,512]{2,1,0:T(8,128)(2,1)} %get-tuple-element.36), channel_id=1, source_target_pairs={{0,2},{2,4},{4,6},{6,8},{8,10},{10,12},{12,14},{14,16},{16,18},{18... | collective-permute-start | bytes 98312 | tf_op jit(solution)/shard_map/ppermute | solution.py:12
  97.0 18.4 %collective-permute-start.7 = (bf16[1,32,512]{2,1,0:T(8,128)(2,1)}, bf16[1,32,512]{2,1,0:T(8,128)(2,1)S(1)}, u32[]{:S(2)}, u32[]{:S(2)}) collective-permute-start(bf16[1,32,512]{2,1,0:T(8,128)(2,1)} %get-tuple-element.37), channel_id=1, source_target_pairs={{2,0},{4,2},{6,4},{8,6},{10,8},{12,10},{14,12},{16,14},{18,16},{20... | collective-permute-start | bytes 98312 | tf_op jit(solution)/shard_map/ppermute | solution.py:15
  105.8 7.3 %copy-start.7 = (bf16[16,32,512]{2,1,0:T(8,128)(2,1)S(1)}, bf16[16,32,512]{2,1,0:T(8,128)(2,1)}, u32[]{:S(2)}) copy-start(bf16[16,32,512]{2,1,0:T(8,128)(2,1)} %copy-done.6) | copy-start | bytes 1572868
  113.4 2.0 copy-start.9
  120.8 152.5 %all-reduce.11.cloned.1.call-start = ((), (), s32[]{:S(2)}) async-start(), calls=%async_computation.1 | async-start | bytes 2097152 | tf_op jit(solution)/shard_map/psum | solution.py:104
  120.9 2.4 copy-start.17
  120.9 1.9 copy-start.11
  121.4 1.9 copy-start.10
  122.9 1.9 copy-start.12
  123.3 1.9 copy-start.13
  125.7 2.0 copy-start.24
  165.8 333.9 %all-reduce.13.cloned.1.call-start = ((), (), s32[]{:S(2)}) async-start(), calls=%async_computation.2 | async-start | bytes 37748736
  166.1 2.8 copy-start.3
  166.1 3.8 copy-start.4
  188.5 1.7 copy-start.15
  188.5 3.2 copy-start.18
  194.7 1.6 copy-start.21
  200.8 302.0 %copy-start.1 = (bf16[2048,256]{1,0:T(8,128)(2,1)S(1)}, bf16[2048,256]{1,0:T(8,128)(2,1)}, u32[]{:S(2)}) copy-start(bf16[2048,256]{1,0:T(8,128)(2,1)} %param.6) | copy-start | bytes 3145732
  (6 other events, 7.7 us)
Sparse Core Ops, SparseCore 0:
  120.9 37.8 all-gather.1
  166.0 107.2 all-reduce.10
  278.8 220.8 all-reduce.12
where the time goes:
time: 511 us; the launch traced here: 509 us
  waiting for transfers between devices  322 us (63%)
  matrix products  49.1 us (10%)
  blocking collectives  44.1 us (9%)
  local copies, waits for them, and re-layouts  36.6 us (7%)
  starting transfers between devices  27.9 us (5%)
  other arithmetic  15.2 us (3%)
  between operations  14.6 us (3%)
    unnamed x4, waiting for transfers between devices  224 us
    psum x1, waiting for transfers between devices, on_device(): lax.psum(code_terms.astype(jnp.bfloat16), ('space', 'clip'))  70.1 us
    psum x1, blocking collectives, on_device(): summed = lax.psum(partial_value, 'code')  44.1 us
    all_gather x1, waiting for transfers between devices, on_device(): piece = lax.all_gather(grad_embedded, 'code', axis=0, tiled=True)  27.6 us
    another operation x2, local copies, waits for them, and re-layouts, kernel_grad(): return jnp.stack(result)  21.1 us
    ppermute x4, starting transfers between devices, with_halo(): lax.ppermute(lax.slice_in_dim(block, 0, width, axis=dim), axis, backward)  19.9 us
    dot_general x18, matrix products, taps_forward(): jnp.dot(window, kernel[first, second], preferred_element_type=jnp.float32)  17.2 us
    another operation x6, other arithmetic, kernel_grad(): return jnp.stack(result)  13.6 us
  transfers between devices with their start and end apart: 11, of which 3 were waited for; matrix products, arithmetic and copies ran while one was open for 13% of the time, Pallas kernels for 0%

commit v1 on v0

--- a/solution.py
+++ b/solution.py
@@ -82,7 +82,7 @@
         weights.reshape(-1, code_slice), codebook, preferred_element_type=jnp.float32
     )
     partial_value = partial_value.reshape(weights.shape[0], breadth, -1)
-    summed = lax.psum(partial_value, "code")
+    summed = jnp.sum(lax.all_gather(partial_value, "code"), axis=0)
     owned = lax.dynamic_slice_in_dim(summed, lax.axis_index("code") * own_rows, own_rows, 0)
     embedded = owned.astype(jnp.bfloat16)
     embed_pad = extend(embedded)

time: 511 us -> 544 us (1.065)
  waiting for transfers between devices: 322 us -> 386 us
  blocking collectives: 44.1 us -> 0 us
  other arithmetic: 15.2 us -> 20.8 us
    all_gather x0 -> x1, waiting for transfers between devices: none -> 68.7 us  [on_device(): summed = jnp.sum(lax.all_gather(partial_value, 'code'), axis=0)]
    psum x1 -> x0, blocking collectives: 44.1 us -> none  [on_device(): summed = lax.psum(partial_value, 'code')]
    all_gather x1, waiting for transfers between devices: 27.6 us -> 21.7 us  [on_device(): piece = lax.all_gather(grad_embedded, 'code', axis=0, tiled=True)]
    reduce_sum x0 -> x1, other arithmetic: none -> 5.64 us  [on_device(): summed = jnp.sum(lax.all_gather(partial_value, 'code'), axis=0)]
    unnamed x59 -> x49, local copies, waits for them, and re-layouts: 9.85 us -> 14.1 us
    unnamed x4 -> x5, waiting for transfers between devices: 224 us -> 224 us
  transfers between devices with their start and end apart: 11 -> 12, of which waited for: 3 -> 5; matrix products, arithmetic and copies ran while one was open for 13% -> 13% of each run, Pallas kernels for 0% -> 0%
where the time goes in v1:
time: 544 us; the launch traced here: 542 us
  waiting for transfers between devices  386 us (71%)
  matrix products  52.9 us (10%)
  local copies, waits for them, and re-layouts  38.9 us (7%)
  starting transfers between devices  29.7 us (5%)
  other arithmetic  20.8 us (4%)
  between operations  14.5 us (3%)
    unnamed x5, waiting for transfers between devices  224 us
    psum x1, waiting for transfers between devices, on_device(): lax.psum(code_terms.astype(jnp.bfloat16), ('space', 'clip'))  70.3 us
    all_gather x1, waiting for transfers between devices, on_device(): summed = jnp.sum(lax.all_gather(partial_value, 'code'), axis=0)  68.7 us
    all_gather x1, waiting for transfers between devices, on_device(): piece = lax.all_gather(grad_embedded, 'code', axis=0, tiled=True)  21.7 us
    another operation x2, local copies, waits for them, and re-layouts, kernel_grad(): return jnp.stack(result)  20.9 us
    ppermute x4, starting transfers between devices, with_halo(): lax.ppermute(lax.slice_in_dim(block, 0, width, axis=dim), axis, backward)  18.1 us
    dot_general x18, matrix products, taps_forward(): jnp.dot(window, kernel[first, second], preferred_element_type=jnp.float32)  17.2 us
    unnamed x49, local copies, waits for them, and re-layouts  14.1 us
  transfers between devices with their start and end apart: 12, of which 5 were waited for; matrix products, arithmetic and copies ran while one was open for 13% of the time, Pallas kernels for 0%

profile of v1, /device:TPU:1, one launch (start us, length us, event | category | flops | bytes accessed | tf_op | source)
XLA Modules:
  0.0 542.3 jit_solution(2941947368784613855)
XLA Ops:
  8.4 7.1 %fusion = f32[64,32,256]{2,1,0:T(8,128)} fusion(bf16[1,64,32,2048]{3,2,1,0:T(8,128)(2,1)} %param.5, bf16[2048,256]{1,0:T(8,128)(2,1)S(1)} %copy-done), kind=kOutput, calls=%fused_computation.1 | convolution fusion | flops 2147483648 | bytes 11534336 | tf_op jit(solution)/shard_map/dot_general | solution.py:81
  15.6 4.4 collective-permute-start.4
  19.9 4.6 collective-permute-start.5
  26.4 2.1 copy-done.3
  33.3 68.7 %all-gather.6.cloned.1.call-done = f32[256,32,256]{2,1,0:T(8,128)} async-done(((f32[64,32,256]{2,1,0:T(8,128)}), f32[256,32,256]{2,1,0:T(8,128)}) %all-gather.6.cloned.1.call-update) | async-done | bytes 8388624 | tf_op jit(solution)/shard_map/all_gather | solution.py:85
  102.0 5.6 %reduce_sum.9 = bf16[64,32,256]{2,1,0:T(8,128)(2,1)} reduce(f32[4,64,32,256]{3,2,1,0:T(8,128)} %bitcast.277, f32[]{:T(128)} %constant.4.clone.1), dimensions={0}, to_apply=%region_0.0 | reduce | flops 1572864 | bytes 9437188 | tf_op jit(solution)/shard_map/reduce_sum | solution.py:85
  108.6 3.0 collective-permute-start
  111.6 3.8 collective-permute-start.1
  115.4 1.9 fusion.4
  117.6 1.6 copy-done.6
  122.0 1.5 convolution_bitcast_fusion.4
  126.4 1.9 collective-permute-start.2
  128.3 4.9 collective-permute-start.3
  133.2 1.9 collective-permute-start.6
  135.1 4.9 collective-permute-start.7
  141.1 2.7 pad_maximum_fusion.1
  143.7 7.2 %copy.12 = f32[3,3,256,512]{2,1,0,3:T(4,128)} copy(f32[3,3,256,512]{3,2,1,0:T(8,128)} %pad_maximum_fusion.1) | data formatting | bytes 9437184 | tf_op jit(solution)/shard_map/stack | solution.py:72
  151.2 1.6 fusion.114
  166.7 3.4 maximum_bitcast_fusion
  170.1 21.7 %all-gather.4.cloned.1.call-done = bf16[64,32,256]{2,1,0:T(8,128)(2,1)} async-done(((bf16[16,32,256]{2,1,0:T(8,128)(2,1)}), bf16[64,32,256]{2,1,0:T(8,128)(2,1)}) %all-gather.4.cloned.1.call-update) | async-done | bytes 1048592 | tf_op jit(solution)/shard_map/all_gather | solution.py:97
  191.8 7.0 %fusion.2 = bf16[2048,256]{0,1:T(8,128)(2,1)} fusion(bf16[2048,256]{1,0:T(8,128)(2,1)} %bitcast.297, bf16[2048,2048]{1,0:T(8,128)(2,1)} %bitcast.276), kind=kOutput, calls=%fused_computation.8 | convolution fusion | flops 2148007936 | bytes 10485760 | tf_op jit(solution)/shard_map/dot_general | solution.py:98
  199.1 2.3 maximum_bitcast_fusion.2
  202.9 4.7 pad_maximum_fusion
  207.6 13.7 %copy.13 = f32[3,3,512,512]{2,1,0,3:T(4,128)} copy(f32[3,3,512,512]{3,2,1,0:T(8,128)} %pad_maximum_fusion) | data formatting | bytes 18874368 | tf_op jit(solution)/shard_map/stack | solution.py:72
  221.3 1.7 fusion.32
  227.5 1.6 convolution_add_fusion.11
  229.1 1.5 convolution_add_fusion.10
  232.1 1.5 convolution_add_fusion.8
  233.6 2.4 fusion.7
  236.0 70.3 %all-reduce.10.cloned.1.call-done = bf16[2048,256]{0,1:T(8,128)(2,1)} async-done(((bf16[2048,256]{0,1:T(8,128)(2,1)}), bf16[2048,256]{0,1:T(8,128)(2,1)}) %all-reduce.10.cloned.1.call-update) | async-done | bytes 1048592 | tf_op jit(solution)/shard_map/psum | solution.py:104
  306.3 2.6 copy.16
  308.8 223.9 %all-reduce.12.cloned.1.call-done = (f32[3,3,256,512]{2,1,0,3:T(4,128)}, f32[3,3,512,512]{2,1,0,3:T(4,128)}) async-done(((f32[3,3,256,512]{2,1,0,3:T(4,128)}, f32[3,3,512,512]{2,1,0,3:T(4,128)}), (f32[3,3,256,512]{2,1,0,3:T(4,128)}, f32[3,3,512,512]{2,1,0,3:T(4,128)})) %all-reduce.12.cloned.1.call-update) | async-done | bytes 14155792
  (128 shorter events, 40.3 us)
Async XLA Ops:
  7.2 1.2 copy-start
  7.2 8.3 %copy-start.2 = (bf16[1,16,32,512]{3,2,1,0:T(8,128)(2,1)S(1)}, bf16[1,16,32,512]{3,2,1,0:T(8,128)(2,1)}, u32[]{:S(2)}) copy-start(bf16[1,16,32,512]{3,2,1,0:T(8,128)(2,1)} %param.9) | copy-start | bytes 1572868
  7.2 94.8 %all-gather.6.cloned.1.call-start = ((), (), s32[]{:S(2)}) async-start(), calls=%async_computation.2 | async-start | bytes 10485760 | tf_op jit(solution)/shard_map/all_gather | solution.py:85
  15.5 176.3 %all-gather.4.cloned.1.call-start = ((), (), s32[]{:S(2)}) async-start(), calls=%async_computation | async-start | bytes 1310720 | tf_op jit(solution)/shard_map/all_gather | solution.py:97
  15.6 9.0 %collective-permute-start.4 = (bf16[1,32,512]{2,1,0:T(8,128)(2,1)S(1)}, bf16[1,32,512]{2,1,0:T(8,128)(2,1)S(1)}, u32[]{:S(2)}, u32[]{:S(2)}) collective-permute-start(bf16[1,32,512]{2,1,0:T(8,128)(2,1)S(1)} %get-tuple-element.40), channel_id=1, source_target_pairs={{0,2},{2,4},{4,6},{6,8},{8,10},{10,12},{12,14},{14,16},{16,18},{18... | collective-permute-start | bytes 98312 | tf_op jit(solution)/shard_map/ppermute | solution.py:12
  19.9 5.6 %collective-permute-start.5 = (bf16[1,32,512]{2,1,0:T(8,128)(2,1)S(1)}, bf16[1,32,512]{2,1,0:T(8,128)(2,1)S(1)}, u32[]{:S(2)}, u32[]{:S(2)}) collective-permute-start(bf16[1,32,512]{2,1,0:T(8,128)(2,1)S(1)} %get-tuple-element.41), channel_id=1, source_target_pairs={{2,0},{4,2},{6,4},{8,6},{10,8},{12,10},{14,12},{16,14},{18,16},{20... | collective-permute-start | bytes 98312 | tf_op jit(solution)/shard_map/ppermute | solution.py:15
  25.9 2.6 copy-start.3
  108.6 8.7 %collective-permute-start = (bf16[1,32,256]{2,1,0:T(8,128)(2,1)S(1)}, bf16[1,32,256]{2,1,0:T(8,128)(2,1)S(1)}, u32[]{:S(2)}, u32[]{:S(2)}) collective-permute-start(bf16[1,32,256]{2,1,0:T(8,128)(2,1)S(1)} %get-tuple-element.54), channel_id=1, source_target_pairs={{0,2},{2,4},{4,6},{6,8},{8,10},{10,12},{12,14},{14,16},{16,18},{18... | collective-permute-start | bytes 49160 | tf_op jit(solution)/shard_map/ppermute | solution.py:12
  111.6 5.7 %collective-permute-start.1 = (bf16[1,32,256]{2,1,0:T(8,128)(2,1)S(1)}, bf16[1,32,256]{2,1,0:T(8,128)(2,1)S(1)}, u32[]{:S(2)}, u32[]{:S(2)}) collective-permute-start(bf16[1,32,256]{2,1,0:T(8,128)(2,1)S(1)} %get-tuple-element.55), channel_id=1, source_target_pairs={{2,0},{4,2},{6,4},{8,6},{10,8},{12,10},{14,12},{16,14},{18,16},{20... | collective-permute-start | bytes 49160 | tf_op jit(solution)/shard_map/ppermute | solution.py:15
  117.2 6.4 %copy-start.19 = (f32[512,512]{1,0:T(8,128)}, f32[512,512]{1,0:T(8,128)S(1)}, u32[]{:S(2)}) copy-start(f32[512,512]{1,0:T(8,128)S(1)} %fusion.4) | copy-start | bytes 3145732
  117.2 2.0 copy-start.6
  122.0 1.6 copy-start.16
  126.4 24.5 %collective-permute-start.2 = (bf16[1,32,512]{2,1,0:T(8,128)(2,1)S(1)}, bf16[1,32,512]{2,1,0:T(8,128)(2,1)S(1)}, u32[]{:S(2)}, u32[]{:S(2)}) collective-permute-start(bf16[1,32,512]{2,1,0:T(8,128)(2,1)S(1)} %get-tuple-element.44), channel_id=1, source_target_pairs={{0,2},{2,4},{4,6},{6,8},{8,10},{10,12},{12,14},{14,16},{16,18},{18... | collective-permute-start | bytes 98312 | tf_op jit(solution)/shard_map/ppermute | solution.py:12
  128.3 22.6 %collective-permute-start.3 = (bf16[1,32,512]{2,1,0:T(8,128)(2,1)S(1)}, bf16[1,32,512]{2,1,0:T(8,128)(2,1)S(1)}, u32[]{:S(2)}, u32[]{:S(2)}) collective-permute-start(bf16[1,32,512]{2,1,0:T(8,128)(2,1)S(1)} %get-tuple-element.45), channel_id=1, source_target_pairs={{2,0},{4,2},{6,4},{8,6},{10,8},{12,10},{14,12},{16,14},{18,16},{20... | collective-permute-start | bytes 98312 | tf_op jit(solution)/shard_map/ppermute | solution.py:15
  133.2 19.6 %collective-permute-start.6 = (bf16[1,32,512]{2,1,0:T(8,128)(2,1)S(1)}, bf16[1,32,512]{2,1,0:T(8,128)(2,1)S(1)}, u32[]{:S(2)}, u32[]{:S(2)}) collective-permute-start(bf16[1,32,512]{2,1,0:T(8,128)(2,1)S(1)} %get-tuple-element.36), channel_id=1, source_target_pairs={{0,2},{2,4},{4,6},{6,8},{8,10},{10,12},{12,14},{14,16},{16,18},{18... | collective-permute-start | bytes 98312 | tf_op jit(solution)/shard_map/ppermute | solution.py:12
  135.1 17.7 %collective-permute-start.7 = (bf16[1,32,512]{2,1,0:T(8,128)(2,1)S(1)}, bf16[1,32,512]{2,1,0:T(8,128)(2,1)S(1)}, u32[]{:S(2)}, u32[]{:S(2)}) collective-permute-start(bf16[1,32,512]{2,1,0:T(8,128)(2,1)S(1)} %get-tuple-element.37), channel_id=1, source_target_pairs={{2,0},{4,2},{6,4},{8,6},{10,8},{12,10},{14,12},{16,14},{18,16},{20... | collective-permute-start | bytes 98312 | tf_op jit(solution)/shard_map/ppermute | solution.py:15
  153.1 1.7 copy-start.7
  155.2 1.2 copy-start.17
  155.2 1.5 copy-start.20
  159.4 146.9 %all-reduce.10.cloned.1.call-start = ((), (), s32[]{:S(2)}) async-start(), calls=%async_computation.1 | async-start | bytes 2097152 | tf_op jit(solution)/shard_map/psum | solution.py:104
  159.5 2.3 copy-start.8
  161.8 1.9 copy-start.9
  162.3 1.9 copy-start.10
  164.2 1.1 copy-start.11
  164.7 2.0 copy-start.21
  198.8 333.9 %all-reduce.12.cloned.1.call-start = ((), (), s32[]{:S(2)}) async-start(), calls=%async_computation.3 | async-start | bytes 37748736
  199.1 2.8 copy-start.4
  199.1 3.8 copy-start.5
  221.3 1.7 copy-start.12
  221.3 3.2 copy-start.15
  227.5 1.6 copy-start.18
  233.6 302.1 %copy-start.1 = (bf16[2048,256]{1,0:T(8,128)(2,1)S(1)}, bf16[2048,256]{1,0:T(8,128)(2,1)}, u32[]{:S(2)}) copy-start(bf16[2048,256]{1,0:T(8,128)(2,1)} %param.6) | copy-start | bytes 3145732
  (2 other events, 1.9 us)
Sparse Core Ops, SparseCore 0:
  15.6 86.3 all-gather.5
  159.5 32.2 all-gather.3
  198.9 107.2 all-reduce.9
  311.7 220.9 all-reduce.11
